TPU v7x, 32 devices: a whole 2x2x4 slice. The times are simulated.
32 devices in a mesh: ent: 8 (over z, y), rep: 4 (over x, core).
Axes of the slice: x: 2, y: 2, z: 4, core: 2. Of those that a mesh axis runs over, the one named last changes fastest.
Arguments:
- facts: bfloat16 [65536, 512], P(('ent', 'rep')), may hold values from -6 to 6
- fact_owner: int32 [65536, 1], P(('ent', 'rep')), may hold values from 0 to 7; in each aligned block of 2048 rows (0 to 2047, 2048 to 4095, ...) at most 512 rows name the same one
- fact_slot: int32 [65536], P(('ent', 'rep')), may hold values from 0 to 127
- entity_feats: bfloat16 [1024, 512], P('ent'), may hold values from -6 to 6
- out_cotangent: bfloat16 [1024, 512], P('ent'), may hold values from -6 to 6
- w_msg: bfloat16 [512, 512], replicated, may hold values from -0.25 to 0.25
- w_upd: bfloat16 [512, 512], replicated, may hold values from -0.25 to 0.25
Outputs:
- ent_out: bfloat16 [1024, 512], P('ent')
- fact_grad: bfloat16 [65536, 512], P(('ent', 'rep'))
- msg_weight_grad: float32 [512, 512], P(('ent', 'rep'))
- upd_weight_grad_t: float32 [512, 512], P(('ent', 'rep'))
Inputs may be any that keep to these rules, and one draw needn't show every extreme that they name: `fact_owner`: among the rows of one device, at most 512 name the same owner.
All inputs are finite; a program needn't handle non-finite values.
Results may differ from a plain program's by a relative error of at most 0.0065.
Values may be sent and summed in bfloat16 or wider, within the bound.
A program may use at most 64 MiB of HBM per device.

v0:
```python
import jax
import jax.numpy as jnp
from jax import lax
from jax.sharding import PartitionSpec as P


def silu_grad(value):
    sig = jax.nn.sigmoid(value)
    return sig * (1.0 + value * (1.0 - sig))


def per_device(facts, fact_owner, fact_slot, entity_feats, out_cotangent, w_msg, w_upd):
    n_owners = lax.axis_size("ent")
    n_copies = lax.axis_size("rep")
    width = facts.shape[1]
    ent_rows = entity_feats.shape[0]
    ents = ent_rows * n_owners
    share = ent_rows // n_copies
    key = fact_owner[:, 0] * ent_rows + fact_slot
    onehot = (jnp.arange(ents, dtype=jnp.int32)[:, None] == key[None, :]).astype(jnp.bfloat16)
    pre = jnp.dot(facts, w_msg, preferred_element_type=jnp.float32)
    message = jax.nn.silu(pre).astype(jnp.bfloat16)
    part_agg = jnp.dot(onehot, message, preferred_element_type=jnp.float32)
    part_count = jnp.sum(onehot, axis=1, dtype=jnp.float32)
    part = jnp.concatenate([part_agg, jnp.broadcast_to(part_count[:, None], (ents, 128))], axis=1)
    both = lax.psum_scatter(part, ("ent", "rep"), scatter_dimension=0, tiled=True)
    agg = both[:, :width]
    denom = jnp.maximum(both[:, width : width + 1], 1.0)
    begin = lax.axis_index("rep") * share
    feats = lax.dynamic_slice_in_dim(entity_feats, begin, share, 0)
    cot = lax.dynamic_slice_in_dim(out_cotangent, begin, share, 0)
    mean = (agg / denom).astype(jnp.bfloat16)
    zval = jnp.dot(mean, w_upd, preferred_element_type=jnp.float32)
    ent_part = (feats.astype(jnp.float32) + jax.nn.silu(zval)).astype(jnp.bfloat16)
    grad_z = (cot.astype(jnp.float32) * silu_grad(zval)).astype(jnp.bfloat16)
    d_mean = lax.dot_general(
        grad_z, w_upd, (((1,), (1,)), ((), ())), preferred_element_type=jnp.float32
    )
    d_agg = (d_mean / denom).astype(jnp.bfloat16)
    d_all = lax.all_gather(d_agg, ("ent", "rep"), axis=0, tiled=True)
    ent_out = lax.all_gather(ent_part, "rep", axis=0, tiled=True)
    d_msg = lax.dot_general(
        onehot, d_all, (((0,), (0,)), ((), ())), preferred_element_type=jnp.float32
    )
    d_pre = (d_msg * silu_grad(pre)).astype(jnp.bfloat16)
    fact_grad = lax.dot_general(
        d_pre, w_msg, (((1,), (1,)), ((), ())), preferred_element_type=jnp.float32
    ).astype(jnp.bfloat16)
    left = lax.dot_general(
        facts, d_pre, (((0,), (0,)), ((), ())), preferred_element_type=jnp.float32
    )
    right = lax.dot_general(
        grad_z, mean, (((0,), (0,)), ((), ())), preferred_element_type=jnp.float32
    )
    grads = lax.psum_scatter(
        jnp.concatenate([left, right], axis=1), ("ent", "rep"), scatter_dimension=0, tiled=True
    )
    return (ent_out, fact_grad, grads[:, :width], grads[:, width:])


def solution(mesh):
    placed = (
        P(("ent", "rep"), None),
        P(("ent", "rep"), None),
        P(("ent", "rep")),
        P("ent", None),
        P("ent", None),
        P(),
        P(),
    )
    return jax.shard_map(
        per_device,
        mesh=mesh,
        in_specs=placed,
        out_specs=(
            P("ent", None),
            P(("ent", "rep"), None),
            P(("ent", "rep"), None),
            P(("ent", "rep"), None),
        ),
        check_vma=False,
    )
```

profile of v0, /device:TPU:0, one launch (start us, length us, event | category | flops | bytes accessed | tf_op | source)
XLA Modules:
  0.0 369.4 jit_solution(3396001357918936834)
XLA Ops:
  7.2 0.8 broadcast_multiply_fusion
  8.1 0.7 add.31
  8.8 0.9 convert_reduce_fusion
  9.7 2.3 fusion.13
  12.0 2.8 fusion.2
  14.9 1.9 pad_maximum_fusion
  16.8 3.3 copy.19
  20.2 140.3 %reduce-scatter.7.cloned.1.call-done = f32[32,640]{1,0:T(8,128)} async-done(((f32[1024,640]{1,0:T(8,128)}), f32[32,640]{1,0:T(8,128)}) %reduce-scatter.7.cloned.1.call-update) | async-done | bytes 81936 | tf_op jit(solution)/shard_map/reduce_scatter | solution.py:26
  160.5 0.7 slice_maximum_fusion
  161.2 0.1 copy.26
  161.3 1.1 add_convert_fusion
  162.4 0.9 fusion.5
  163.4 1.3 fusion.8
  164.6 48.9 %all-gather.2.cloned.1.call-done = bf16[1024,512]{1,0:T(8,128)(2,1)} async-done(((bf16[32,512]{1,0:T(8,128)(2,1)}), bf16[1024,512]{1,0:T(8,128)(2,1)}) %all-gather.2.cloned.1.call-update) | async-done | bytes 1048592 | tf_op jit(solution)/shard_map/all_gather | solution.py:40
  213.5 6.1 %multiply_convert_fusion = bf16[2048,512]{1,0:T(8,128)(2,1)S(1)} fusion(f32[2048,512]{1,0:T(8,128)} %copy-done.1, bf16[1024,512]{1,0:T(8,128)(2,1)} %all-gather.2.cloned.1.call-done, s32[2048]{0:T(1024)S(1)} %add.31), kind=kOutput, calls=%fused_computation.5 | convolution fusion | flops 2159017984 | bytes 7348224 | tf_op jit(solution)/shard_map/dot_general | solution.py:42
  219.6 1.3 convolution_bitcast_fusion
  220.9 0.0 copy-done.5
  221.0 1.5 pad_maximum_fusion.1
  222.4 2.9 copy.21
  225.4 5.4 %all_gather.6 = bf16[128,512]{1,0:T(8,128)(2,1)S(1)} all-gather(bf16[32,512]{1,0:T(8,128)(2,1)S(1)} %get-tuple-element.18), channel_id=1, replica_groups=mesh['ent'=8,'rep'=4] {'rep'}, dimensions={0}, use_global_device_ids=true | all-gather | bytes 163840 | tf_op jit(solution)/shard_map/all_gather | solution.py:41
  230.8 4.2 %convolution_convert_fusion = bf16[2048,512]{1,0:T(8,128)(2,1)} fusion(bf16[2048,512]{1,0:T(8,128)(2,1)} %copy-done.5, bf16[512,512]{1,0:T(8,128)(2,1)S(1)} %copy-done.2), kind=kOutput, calls=%fused_computation.10 | convolution fusion | flops 1074790400 | bytes 4718592 | tf_op jit(solution)/shard_map/dot_general | solution.py:46
  235.0 125.8 %reduce-scatter.9.cloned.1.call-done = f32[16,1024]{1,0:T(8,128)} async-done(((f32[512,1024]{1,0:T(8,128)}), f32[16,1024]{1,0:T(8,128)}) %reduce-scatter.9.cloned.1.call-update) | async-done | bytes 65552
  360.8 1.4 fusion.12
  362.2 0.7 copy.28
  (18 shorter events, 0.2 us)
Async XLA Ops:
  7.2 2.5 copy-start
  7.2 153.3 %reduce-scatter.7.cloned.1.call-start = ((), (), s32[]{:S(2)}) async-start(), calls=%async_computation.3 | async-start | bytes 2703360 | tf_op jit(solution)/shard_map/reduce_scatter | solution.py:26
  12.0 2.8 copy-start.1
  20.1 141.2 %copy-start.4 = (bf16[512,512]{1,0:T(8,128)(2,1)S(1)}, bf16[512,512]{1,0:T(8,128)(2,1)}, u32[]{:S(2)}) copy-start(bf16[512,512]{1,0:T(8,128)(2,1)} %param.13) | copy-start | bytes 1572868
  20.1 142.3 %copy-start.3 = (bf16[128,512]{1,0:T(8,128)(2,1)S(1)}, bf16[128,512]{1,0:T(8,128)(2,1)}, u32[]{:S(2)}) copy-start(bf16[128,512]{1,0:T(8,128)(2,1)} %param.11) | copy-start | bytes 393220
  20.1 193.4 %all-gather.2.cloned.1.call-start = ((), (), s32[]{:S(2)}) async-start(), calls=%async_computation.2 | async-start | bytes 1081344 | tf_op jit(solution)/shard_map/all_gather | solution.py:40
  163.3 197.5 %reduce-scatter.9.cloned.1.call-start = ((), (), s32[]{:S(2)}) async-start(), calls=%async_computation.4 | async-start | bytes 2162688
  219.6 1.3 copy-start.5
  222.4 8.4 %copy-start.2 = (bf16[512,512]{1,0:T(8,128)(2,1)S(1)}, bf16[512,512]{1,0:T(8,128)(2,1)}, u32[]{:S(2)}) copy-start(bf16[512,512]{1,0:T(8,128)(2,1)} %param.12) | copy-start | bytes 1572868
Sparse Core Ops, SparseCore 0:
  20.2 140.2 reduce-scatter.6
  163.9 49.5 all-gather.1
  225.5 135.2 reduce-scatter.8
where the time goes:
time: 370 us; the launch traced here: 369 us
  waiting for transfers between devices  315 us (85%)
  matrix products  19.9 us (5%)
  between operations  13.8 us (4%)
  local copies, waits for them, and re-layouts  8.47 us (2%)
  other arithmetic  6.59 us (2%)
  blocking collectives  5.43 us (1%)
    reduce_scatter x1, waiting for transfers between devices, per_device(): lax.psum_scatter(part, ('ent', 'rep'), scatter_dimension=0, tiled=True)  140 us
    unnamed x4, waiting for transfers between devices  126 us
    all_gather x1, waiting for transfers between devices, per_device(): d_all = lax.all_gather(d_agg, ('ent', 'rep'), axis=0, tiled=True)  48.9 us
  transfers between devices with their start and end apart: 3, of which 3 were waited for; matrix products, arithmetic and copies ran while one was open for 1% of the time, Pallas kernels for 0%

commit v1 on v0

--- a/solution.py
+++ b/solution.py
@@ -2,6 +2,18 @@
 import jax.numpy as jnp
 from jax import lax
 from jax.sharding import PartitionSpec as P
+
+
+def gather_by_bits(x, axis, dim):
+    ways, here = (lax.axis_size(axis), lax.axis_index(axis))
+    grown, reach = (x, 1)
+    while reach < ways:
+        theirs = lax.ppermute(grown, axis, [(d, d ^ reach) for d in range(ways)])
+        mine_first = jnp.concatenate([grown, theirs], axis=dim)
+        theirs_first = jnp.concatenate([theirs, grown], axis=dim)
+        grown = jnp.where(here & reach == 0, mine_first, theirs_first)
+        reach = 2 * reach
+    return grown
 
 
 def silu_grad(value):
@@ -37,7 +49,7 @@
         grad_z, w_upd, (((1,), (1,)), ((), ())), preferred_element_type=jnp.float32
     )
     d_agg = (d_mean / denom).astype(jnp.bfloat16)
-    d_all = lax.all_gather(d_agg, ("ent", "rep"), axis=0, tiled=True)
+    d_all = gather_by_bits(d_agg, ("ent", "rep"), 0)
     ent_out = lax.all_gather(ent_part, "rep", axis=0, tiled=True)
     d_msg = lax.dot_general(
         onehot, d_all, (((0,), (0,)), ((), ())), preferred_element_type=jnp.float32

time: 370 us -> 360 us (0.973)
  waiting for transfers between devices: 315 us -> 304 us
    all_gather x1 -> x0, waiting for transfers between devices: 48.9 us -> none  [per_device(): d_all = lax.all_gather(d_agg, ('ent', 'rep'), axis=0, tiled=True)]
    ppermute x0 -> x5, waiting for transfers between devices: none -> 38.7 us  [gather_by_bits(): theirs = lax.ppermute(grown, axis, [(d, d ^ reach) for d in range(ways)])]
    unnamed x4 -> x3, waiting for transfers between devices: 126 us -> 125 us
  transfers between devices with their start and end apart: 3 -> 7, of which waited for: 3 -> 7; matrix products, arithmetic and copies ran while one was open for 1% -> 1% of each run, Pallas kernels for 0% -> 0%
where the time goes in v1:
time: 360 us
  waiting for transfers between devices  304 us (84%)
  matrix products  19.5 us (5%)
  between operations  14.2 us (4%)
  local copies, waits for them, and re-layouts  8.43 us (2%)
  other arithmetic  6.97 us (2%)
  blocking collectives  5.92 us (2%)
    reduce_scatter x1, waiting for transfers between devices, per_device(): lax.psum_scatter(part, ('ent', 'rep'), scatter_dimension=0, tiled=True)  140 us
    unnamed x3, waiting for transfers between devices  125 us
    ppermute x5, waiting for transfers between devices, gather_by_bits(): theirs = lax.ppermute(grown, axis, [(d, d ^ reach) for d in range(ways)])  38.7 us
  transfers between devices with their start and end apart: 7, of which 7 were waited for; matrix products, arithmetic and copies ran while one was open for 1% of the time, Pallas kernels for 0%

profile of v1, /device:TPU:0, one launch (start us, length us, event | category | flops | bytes accessed | tf_op | source)
XLA Modules:
  0.0 359.8 jit_solution(16743565029354760828)
XLA Ops:
  7.2 0.8 broadcast_multiply_fusion
  8.1 0.7 add.34
  8.8 0.9 convert_reduce_fusion
  9.7 2.3 fusion.20
  12.0 2.8 fusion.2
  14.9 1.9 pad_maximum_fusion
  16.8 3.3 copy.20
  20.2 140.5 %reduce-scatter.7.cloned.1.call-done = f32[32,640]{1,0:T(8,128)} async-done(((f32[1024,640]{1,0:T(8,128)}), f32[32,640]{1,0:T(8,128)}) %reduce-scatter.7.cloned.1.call-update) | async-done | bytes 81936 | tf_op jit(solution)/shard_map/reduce_scatter | solution.py:38
  160.6 0.8 slice_maximum_fusion
  161.5 1.1 add_convert_fusion
  163.0 1.2 collective-permute-done
  164.3 4.2 %collective-permute-done.1 = bf16[64,512]{1,0:T(8,128)(2,1)S(1)} collective-permute-done((bf16[64,512]{1,0:T(8,128)(2,1)S(1)}, bf16[64,512]{1,0:T(8,128)(2,1)S(1)}, u32[]{:S(2)}, u32[]{:S(2)}) %collective-permute-start.1) | collective-permute-done | bytes 65568 | tf_op jit(solution)/shard_map/ppermute | solution.py:11
  168.6 4.9 %collective-permute-done.2 = bf16[128,512]{1,0:T(8,128)(2,1)S(1)} collective-permute-done((bf16[128,512]{1,0:T(8,128)(2,1)S(1)}, bf16[128,512]{1,0:T(8,128)(2,1)S(1)}, u32[]{:S(2)}, u32[]{:S(2)}) %collective-permute-start.2) | collective-permute-done | bytes 131104 | tf_op jit(solution)/shard_map/ppermute | solution.py:11
  173.7 6.4 %collective-permute-done.3 = bf16[256,512]{1,0:T(8,128)(2,1)S(1)} collective-permute-done((bf16[256,512]{1,0:T(8,128)(2,1)S(1)}, bf16[256,512]{1,0:T(8,128)(2,1)S(1)}, u32[]{:S(2)}, u32[]{:S(2)}) %collective-permute-start.3) | collective-permute-done | bytes 262176 | tf_op jit(solution)/shard_map/ppermute | solution.py:11
  180.8 21.9 %collective-permute-done.4 = bf16[512,512]{1,0:T(8,128)(2,1)S(1)} collective-permute-done((bf16[512,512]{1,0:T(8,128)(2,1)S(1)}, bf16[512,512]{1,0:T(8,128)(2,1)S(1)}, u32[]{:S(2)}, u32[]{:S(2)}) %collective-permute-start.4) | collective-permute-done | bytes 524320 | tf_op jit(solution)/shard_map/ppermute | solution.py:11
  202.8 7.1 %multiply_convert_fusion = bf16[2048,512]{1,0:T(8,128)(2,1)S(1)} fusion(f32[2048,512]{1,0:T(8,128)} %copy-done.1, s32[2048]{0:T(1024)S(1)} %add.34, bf16[512,512]{1,0:T(8,128)(2,1)S(1)} %collective-permute-done.4, bf16[512,512]{1,0:T(8,128)(2,1)S(1)} %maximum_select_fusion.2, pred[]{:T(512)S(6)} %eq.31), kind=kOutput, calls=%fused_computation.5 | convolution fusion | flops 2163736576 | bytes 7348225 | tf_op jit(solution)/shard_map/dot_general | solution.py:54
  209.9 1.3 convolution_bitcast_fusion
  211.2 1.5 pad_maximum_fusion.1
  212.7 2.9 copy.22
  215.7 5.9 %all_gather.3 = bf16[128,512]{1,0:T(8,128)(2,1)S(1)} all-gather(bf16[32,512]{1,0:T(8,128)(2,1)S(1)} %get-tuple-element.18), channel_id=1, replica_groups=mesh['ent'=8,'rep'=4] {'rep'}, dimensions={0}, use_global_device_ids=true | all-gather | bytes 163840 | tf_op jit(solution)/shard_map/all_gather | solution.py:53
  221.6 4.2 %convolution_convert_fusion = bf16[2048,512]{1,0:T(8,128)(2,1)} fusion(bf16[2048,512]{1,0:T(8,128)(2,1)} %copy-done.6, bf16[512,512]{1,0:T(8,128)(2,1)S(1)} %copy-done.2), kind=kOutput, calls=%fused_computation.10 | convolution fusion | flops 1074790400 | bytes 4718592 | tf_op jit(solution)/shard_map/dot_general | solution.py:58
  225.8 125.1 %reduce-scatter.9.cloned.1.call-done = f32[16,1024]{1,0:T(8,128)} async-done(((f32[512,1024]{1,0:T(8,128)}), f32[16,1024]{1,0:T(8,128)}) %reduce-scatter.9.cloned.1.call-update) | async-done | bytes 65552
  350.9 1.4 fusion.19
  352.3 0.7 copy.29
  (31 shorter events, 1.6 us)
Async XLA Ops:
  7.2 2.5 copy-start
  7.2 153.5 %reduce-scatter.7.cloned.1.call-start = ((), (), s32[]{:S(2)}) async-start(), calls=%async_computation.2 | async-start | bytes 2703360 | tf_op jit(solution)/shard_map/reduce_scatter | solution.py:38
  12.0 2.8 copy-start.1
  20.1 141.4 %copy-start.5 = (bf16[512,512]{1,0:T(8,128)(2,1)S(1)}, bf16[512,512]{1,0:T(8,128)(2,1)}, u32[]{:S(2)}) copy-start(bf16[512,512]{1,0:T(8,128)(2,1)} %param.13) | copy-start | bytes 1572868
  20.1 142.6 %copy-start.4 = (bf16[128,512]{1,0:T(8,128)(2,1)S(1)}, bf16[128,512]{1,0:T(8,128)(2,1)}, u32[]{:S(2)}) copy-start(bf16[128,512]{1,0:T(8,128)(2,1)} %param.11) | copy-start | bytes 393220
  20.1 330.8 %reduce-scatter.9.cloned.1.call-start = ((), (), s32[]{:S(2)}) async-start(), calls=%async_computation.3 | async-start | bytes 2162688
  160.6 19.7 %copy-start.3 = (f32[32,640]{1,0:T(8,128)S(1)}, f32[32,640]{1,0:T(8,128)}, u32[]{:S(2)}) copy-start(f32[32,640]{1,0:T(8,128)} %reduce-scatter.7.cloned.1.call-done) | copy-start | bytes 245764
  162.9 1.3 collective-permute-start
  164.2 4.3 %collective-permute-start.1 = (bf16[64,512]{1,0:T(8,128)(2,1)S(1)}, bf16[64,512]{1,0:T(8,128)(2,1)S(1)}, u32[]{:S(2)}, u32[]{:S(2)}) collective-permute-start(bf16[64,512]{1,0:T(8,128)(2,1)S(1)} %maximum_select_fusion.5), channel_id=1, source_target_pairs={{0,2},{1,3},{2,0},{3,1},{4,6},{5,7},{6,4},{7,5},{8,10},{9,11},{10,... | collective-permute-start | bytes 196616 | tf_op jit(solution)/shard_map/ppermute | solution.py:11
  168.6 5.0 %collective-permute-start.2 = (bf16[128,512]{1,0:T(8,128)(2,1)S(1)}, bf16[128,512]{1,0:T(8,128)(2,1)S(1)}, u32[]{:S(2)}, u32[]{:S(2)}) collective-permute-start(bf16[128,512]{1,0:T(8,128)(2,1)S(1)} %maximum_select_fusion.4), channel_id=1, source_target_pairs={{0,4},{1,5},{2,6},{3,7},{4,0},{5,1},{6,2},{7,3},{8,12},{9,13},{10,... | collective-permute-start | bytes 393224 | tf_op jit(solution)/shard_map/ppermute | solution.py:11
  173.6 6.4 %collective-permute-start.3 = (bf16[256,512]{1,0:T(8,128)(2,1)S(1)}, bf16[256,512]{1,0:T(8,128)(2,1)S(1)}, u32[]{:S(2)}, u32[]{:S(2)}) collective-permute-start(bf16[256,512]{1,0:T(8,128)(2,1)S(1)} %maximum_select_fusion.3), channel_id=1, source_target_pairs={{0,8},{1,9},{2,10},{3,11},{4,12},{5,13},{6,14},{7,15},{8,0},{9,1},... | collective-permute-start | bytes 786440 | tf_op jit(solution)/shard_map/ppermute | solution.py:11
  180.3 22.5 %collective-permute-start.4 = (bf16[512,512]{1,0:T(8,128)(2,1)S(1)}, bf16[512,512]{1,0:T(8,128)(2,1)S(1)}, u32[]{:S(2)}, u32[]{:S(2)}) collective-permute-start(bf16[512,512]{1,0:T(8,128)(2,1)S(1)} %maximum_select_fusion.2), channel_id=1, source_target_pairs={{0,16},{1,17},{2,18},{3,19},{4,20},{5,21},{6,22},{7,23},{8,24},{9,... | collective-permute-start | bytes 1572872 | tf_op jit(solution)/shard_map/ppermute | solution.py:11
  209.9 1.3 copy-start.6
  215.6 5.9 %copy-start.2 = (bf16[512,512]{1,0:T(8,128)(2,1)S(1)}, bf16[512,512]{1,0:T(8,128)(2,1)}, u32[]{:S(2)}) copy-start(bf16[512,512]{1,0:T(8,128)(2,1)} %param.12) | copy-start | bytes 1572868
Sparse Core Ops, SparseCore 0:
  20.2 140.3 reduce-scatter.6
  215.8 135.0 reduce-scatter.8
